TPU v7x, 32 devices: a whole 2x2x4 slice. The times are simulated.
32 devices in a mesh: groups: 2 (over x), slab: 16 (over z, y, core).
Axes of the slice: x: 2, y: 2, z: 4, core: 2. Of those that a mesh axis runs over, the one named last changes fastest.
Arguments:
- activations: bfloat16 [2048, 65536], P(('groups', 'slab')), parts along dimension 0, may hold values from 0 to 4
- weights: bfloat16 [6, 2, 512, 128, 128], P(None, None, 'slab'), may hold values from -0.5 to 0.5
- biases: float32 [6, 65536], P(None, 'slab'), may hold values from -1 to 0.5
- columns: int32 [6, 512], P(None, 'slab'), may hold values from 0 to 31
Outputs:
- features: bfloat16 [2048, 65536], P(('groups', 'slab')), parts along dimension 0
There are 2 independent parts, one for each index of `groups`. A program takes and returns all parts, laid end to end along the dimension named above; an argument that names none is the same for every part. Nothing has to cross between parts.
Inputs may be any that keep to these rules, and one draw needn't show every extreme that they name: columns name a block within a group of 32 consecutive blocks.
All inputs are finite; a program needn't handle non-finite values.
Results may differ from a plain program's by a relative error of at most 0.0072.
Values may be sent and summed in bfloat16 or wider, within the bound.
No kernel may reach another device: no remote copies, remote signals or barrier semaphores. Data moves between devices by JAX's collectives and lax.ppermute only.
A program may use at most 128 MiB of HBM per device.

v0:
```python
import jax
import jax.numpy as jnp
from jax import lax
from jax.sharding import PartitionSpec as P

ceiling = 4.0


def from_partner(block, axis, bit):
    count = lax.axis_size(axis)
    route = []
    for low in range(count):
        high = low | 1 << bit
        if high != low and high < count:
            route += [(low, high), (high, low)]
    return lax.ppermute(block, axis, route)


def section_bit(section, remote, log_count):
    return (remote - 1 - section) * (log_count - 1) // (remote - 1)


def local(activations, weights, biases, columns):
    slab_count = lax.axis_size("slab")
    log_count = slab_count.bit_length() - 1
    layer_count = weights.shape[0]
    per_device = weights.shape[2]
    block_width = weights.shape[3]
    local_rows = activations.shape[0]
    remote = (layer_count + 1) // 2
    grouped = activations.reshape(local_rows, slab_count, per_device * block_width)
    stride = 1 << section_bit(0, remote, log_count)
    flipped = grouped.reshape(
        local_rows, slab_count // (2 * stride), 2, stride, per_device * block_width
    )
    flipped = flipped[:, :, ::-1].reshape(local_rows, slab_count, per_device * block_width)
    paired = jnp.stack([grouped, flipped], axis=2)
    arrived = lax.all_to_all(paired, "slab", split_axis=1, concat_axis=0, tiled=True)
    current = arrived[:, 0, 0].reshape(-1, per_device, block_width)
    first_cross = arrived[:, 0, 1].reshape(-1, per_device, block_width)
    for layer_index in range(layer_count):
        if layer_index % 2 == 0:
            if layer_index == 0 and first_cross is not None:
                source = first_cross
            else:
                source = from_partner(
                    current, "slab", section_bit(layer_index // 2, remote, log_count)
                )
        else:
            source = current
        crossing = jnp.take(source, columns[layer_index], axis=1)
        summed = jnp.einsum(
            "rkb,kbc->rkc", current, weights[layer_index, 0], preferred_element_type=jnp.float32
        )
        summed = summed + jnp.einsum(
            "rkb,kbc->rkc", crossing, weights[layer_index, 1], preferred_element_type=jnp.float32
        )
        summed = summed + biases[layer_index].reshape(per_device, block_width)
        current = jnp.clip(summed, 0.0, ceiling).astype(jnp.bfloat16)
    flattened = current.reshape(current.shape[0], per_device * block_width)
    return lax.all_to_all(flattened, "slab", split_axis=0, concat_axis=1, tiled=True)


def solution(mesh):
    placed = (
        P(("groups", "slab"), None),
        P(None, None, "slab", None, None),
        P(None, "slab"),
        P(None, "slab"),
    )
    return jax.shard_map(
        local, mesh=mesh, in_specs=placed, out_specs=P(("groups", "slab"), None), check_vma=False
    )
```

profile of v0, /device:TPU:1, one launch (start us, length us, event | category | flops | bytes accessed | tf_op | source)
XLA Modules:
  0.0 1066.5 jit_solution(5412748452448401006)
XLA Ops:
  0.0 12.1 %copy.28 = bf16[8,8,16,4096]{3,2,1,0:T(8,128)(2,1)} copy(bf16[8,8,16,4096]{3,1,2,0:T(8,128)(2,1)} %bitcast.134) | data formatting | bytes 16777216
  12.1 7.7 reverse_bitcast_fusion
  19.9 8.0 pad_maximum_fusion
  27.9 21.4 %copy.18 = bf16[64,16,2,4096]{3,0,2,1:T(8,128)(2,1)} copy(bf16[64,16,2,4096]{3,1,0,2:T(8,128)(2,1)S(1)} %pad_maximum_fusion) | data formatting | bytes 33554432 | tf_op jit(solution)/shard_map/stack | solution.py:37
  49.2 0.0 copy-start.2
  49.2 0.0 copy-start
  49.2 8.1 all-to-all-start
  57.4 0.0 copy-done.2
  57.4 0.5 compare_and_fusion
  57.9 0.0 copy-done
  57.9 0.7 fusion.79
  58.6 295.9 %all-to-all-done = bf16[64,16,2,4096]{3,0,2,1:T(8,128)(2,1)} async-done(((bf16[64,16,2,4096]{3,0,2,1:T(8,128)(2,1)}), bf16[64,16,2,4096]{3,0,2,1:T(8,128)(2,1)}, u32[]{:S(2)}, u32[]{:S(2)}) %all-to-all-start) | async-done | bytes 16777248 | tf_op jit(solution)/shard_map/all_to_all | solution.py:38
  354.5 8.3 copy.19
  362.7 6.4 fusion.78
  369.2 12.0 %copy.22 = bf16[1024,1,1,4096]{0,3,2,1:T(8,128)(2,1)} copy(bf16[1024,1,1,4096]{3,0,2,1:T(8,128)(2,1)} %get-tuple-element.18) | data formatting | bytes 16777216 | tf_op jit(solution)/shard_map/slice | solution.py:40
  381.1 11.4 %copy.23 = bf16[1024,32,128]{2,0,1:T(8,128)(2,1)} copy(bf16[1024,32,128]{0,2,1:T(8,128)(2,1)} %bitcast.132) | data formatting | bytes 16777216 | tf_op jit(solution)/shard_map/reshape;squeeze | solution.py:40
  392.5 11.9 %copy.20 = bf16[1024,1,1,4096]{0,3,2,1:T(8,128)(2,1)} copy(bf16[1024,1,1,4096]{3,0,2,1:T(8,128)(2,1)} %get-tuple-element.19) | data formatting | bytes 16777216 | tf_op jit(solution)/shard_map/slice | solution.py:39
  404.4 8.4 gather_fusion
  412.8 11.8 %fusion.58 = f32[32,1024,128]{2,1,0:T(8,128)} fusion(bf16[1024,32,128]{0,2,1:T(8,128)(2,1)} %bitcast.131, bf16[6,2,32,128,128]{4,3,2,1,0:T(8,128)(2,1)} %param.7), kind=kOutput, calls=%fused_computation.60 | convolution fusion | flops 1073741824 | bytes 26214400 | tf_op jit(solution)/shard_map/rkb,kbc->rkc/dot_general | solution.py:52
  424.6 13.5 %fusion.18 = bf16[1024,32,128]{2,0,1:T(8,128)(2,1)} fusion(f32[32,128]{1,0:T(8,128)S(1)} %bitcast.140, f32[32,1024,128]{2,1,0:T(8,128)} %fusion.58, bf16[32,1024,128]{2,1,0:T(8,128)(2,1)} %gather_fusion, pred[32]{0:T(512)(128)(4,1)S(1)} %get-tuple-element.32, bf16[6,2,32,128,128]{4,3,2,1,0:T(8,128)(2,1)} %param.7), kind=kOutput, calls=%fused_computation.32 | convolution fusion | flops 1094713344 | bytes 34619424 | tf_op jit(solution)/shard_map/rkb,kbc->rkc/dot_general | solution.py:55
  438.2 11.7 %fusion.55 = f32[32,1024,128]{2,1,0:T(8,128)} fusion(bf16[1024,32,128]{2,0,1:T(8,128)(2,1)} %fusion.18, bf16[6,2,32,128,128]{4,3,2,1,0:T(8,128)(2,1)} %param.7), kind=kOutput, calls=%fused_computation.57 | convolution fusion | flops 1073741824 | bytes 26214400 | tf_op jit(solution)/shard_map/rkb,kbc->rkc/dot_general | solution.py:52
  449.8 8.4 gather_fusion.1
  458.2 13.7 %fusion.21 = bf16[1024,32,128]{2,0,1:T(8,128)(2,1)} fusion(f32[32,128]{1,0:T(8,128)S(1)} %bitcast.139, f32[32,1024,128]{2,1,0:T(8,128)} %fusion.55, bf16[32,1024,128]{2,1,0:T(8,128)(2,1)} %gather_fusion.1, pred[32]{0:T(512)(128)(4,1)S(1)} %get-tuple-element.30, bf16[6,2,32,128,128]{4,3,2,1,0:T(8,128)(2,1)} %param.7), kind=kOutput, calls=%fused_computation.33 | convolution fusion | flops 1094713344 | bytes 34619424 | tf_op jit(solution)/shard_map/rkb,kbc->rkc/dot_general | solution.py:55
  471.9 22.8 %collective-permute-start = (bf16[1024,32,128]{2,0,1:T(8,128)(2,1)}, bf16[1024,32,128]{2,0,1:T(8,128)(2,1)}, u32[]{:S(2)}, u32[]{:S(2)}) collective-permute-start(bf16[1024,32,128]{2,0,1:T(8,128)(2,1)} %fusion.21), channel_id=1, source_target_pairs={{0,2},{2,0},{1,3},{3,1},{4,6},{6,4},{5,7},{7,5},{8,10},{10,8},{9,1... | collective-permute-start | bytes 25165832 | tf_op jit(solution)/shard_map/ppermute | solution.py:16
  494.7 11.7 %fusion.52 = f32[32,1024,128]{2,1,0:T(8,128)} fusion(bf16[1024,32,128]{2,0,1:T(8,128)(2,1)} %fusion.21, bf16[6,2,32,128,128]{4,3,2,1,0:T(8,128)(2,1)} %param.7), kind=kOutput, calls=%fused_computation.54 | convolution fusion | flops 1073741824 | bytes 26214400 | tf_op jit(solution)/shard_map/rkb,kbc->rkc/dot_general | solution.py:52
  506.4 169.1 %collective-permute-done = bf16[1024,32,128]{2,0,1:T(8,128)(2,1)} collective-permute-done((bf16[1024,32,128]{2,0,1:T(8,128)(2,1)}, bf16[1024,32,128]{2,0,1:T(8,128)(2,1)}, u32[]{:S(2)}, u32[]{:S(2)}) %collective-permute-start) | collective-permute-done | bytes 8388640 | tf_op jit(solution)/shard_map/ppermute | solution.py:16
  675.5 8.6 gather_fusion.2
  684.1 13.5 %fusion.24 = bf16[1024,32,128]{2,0,1:T(8,128)(2,1)} fusion(f32[32,128]{1,0:T(8,128)S(1)} %bitcast.138, f32[32,1024,128]{2,1,0:T(8,128)} %fusion.52, bf16[32,1024,128]{2,1,0:T(8,128)(2,1)} %gather_fusion.2, pred[32]{0:T(512)(128)(4,1)S(1)} %get-tuple-element.28, bf16[6,2,32,128,128]{4,3,2,1,0:T(8,128)(2,1)} %param.7), kind=kOutput, calls=%fused_computation.34 | convolution fusion | flops 1094713344 | bytes 34619424 | tf_op jit(solution)/shard_map/rkb,kbc->rkc/dot_general | solution.py:55
  697.6 11.7 %fusion.49 = f32[32,1024,128]{2,1,0:T(8,128)} fusion(bf16[1024,32,128]{2,0,1:T(8,128)(2,1)} %fusion.24, bf16[6,2,32,128,128]{4,3,2,1,0:T(8,128)(2,1)} %param.7), kind=kOutput, calls=%fused_computation.51 | convolution fusion | flops 1073741824 | bytes 26214400 | tf_op jit(solution)/shard_map/rkb,kbc->rkc/dot_general | solution.py:52
  709.3 8.5 gather_fusion.3
  717.8 13.5 %fusion.27 = bf16[1024,32,128]{2,0,1:T(8,128)(2,1)} fusion(f32[32,128]{1,0:T(8,128)S(1)} %bitcast.137, f32[32,1024,128]{2,1,0:T(8,128)} %fusion.49, bf16[32,1024,128]{2,1,0:T(8,128)(2,1)} %gather_fusion.3, pred[32]{0:T(512)(128)(4,1)S(1)} %get-tuple-element.26, bf16[6,2,32,128,128]{4,3,2,1,0:T(8,128)(2,1)} %param.7), kind=kOutput, calls=%fused_computation.35 | convolution fusion | flops 1094713344 | bytes 34619424 | tf_op jit(solution)/shard_map/rkb,kbc->rkc/dot_general | solution.py:55
  731.3 0.4 collective-permute-start.1
  731.7 11.7 %fusion.46 = f32[32,1024,128]{2,1,0:T(8,128)} fusion(bf16[1024,32,128]{2,0,1:T(8,128)(2,1)} %fusion.27, bf16[6,2,32,128,128]{4,3,2,1,0:T(8,128)(2,1)} %param.7), kind=kOutput, calls=%fused_computation.48 | convolution fusion | flops 1073741824 | bytes 26214400 | tf_op jit(solution)/shard_map/rkb,kbc->rkc/dot_general | solution.py:52
  743.4 1.4 collective-permute-done.1
  744.8 8.8 gather_fusion.4
  753.6 13.5 %fusion.30 = bf16[1024,32,128]{2,0,1:T(8,128)(2,1)} fusion(f32[32,128]{1,0:T(8,128)S(1)} %bitcast.136, f32[32,1024,128]{2,1,0:T(8,128)} %fusion.46, bf16[32,1024,128]{2,1,0:T(8,128)(2,1)} %gather_fusion.4, pred[32]{0:T(512)(128)(4,1)S(1)} %get-tuple-element.34, bf16[6,2,32,128,128]{4,3,2,1,0:T(8,128)(2,1)} %param.7), kind=kOutput, calls=%fused_computation.36 | convolution fusion | flops 1094713344 | bytes 34619424 | tf_op jit(solution)/shard_map/rkb,kbc->rkc/dot_general | solution.py:55
  767.1 11.7 %fusion.43 = f32[32,1024,128]{2,1,0:T(8,128)} fusion(bf16[1024,32,128]{2,0,1:T(8,128)(2,1)} %fusion.30, bf16[6,2,32,128,128]{4,3,2,1,0:T(8,128)(2,1)} %param.7), kind=kOutput, calls=%fused_computation.45 | convolution fusion | flops 1073741824 | bytes 26214400 | tf_op jit(solution)/shard_map/rkb,kbc->rkc/dot_general | solution.py:52
  778.8 0.0 copy-start.1
  778.8 0.0 copy-start.3
  778.8 8.6 gather_fusion.5
  787.4 0.0 copy-done.1
  787.4 0.0 copy-done.3
  787.4 13.7 %fusion.33 = bf16[1024,32,128]{2,0,1:T(8,128)(2,1)} fusion(f32[32,128]{1,0:T(8,128)S(1)} %bitcast.135, f32[32,1024,128]{2,1,0:T(8,128)} %fusion.43, bf16[32,1024,128]{2,1,0:T(8,128)(2,1)} %gather_fusion.5, pred[32]{0:T(512)(128)(4,1)S(1)} %copy-done.3, bf16[6,2,32,128,128]{4,3,2,1,0:T(8,128)(2,1)} %param.7), kind=kOutput, calls=%fused_computation.37 | convolution fusion | flops 1094713344 | bytes 34619424 | tf_op jit(solution)/shard_map/rkb,kbc->rkc/dot_general | solution.py:55
  801.1 12.2 %copy.24 = bf16[1024,32,128]{2,1,0:T(8,128)(2,1)} copy(bf16[1024,32,128]{2,0,1:T(8,128)(2,1)} %fusion.33) | data formatting | bytes 16777216 | tf_op jit(solution)/shard_map/convert_element_type | solution.py:59
  813.3 13.3 %all_to_all.31 = bf16[16,64,4096]{2,1,0:T(8,128)(2,1)} reshape(bf16[1024,32,128]{2,1,0:T(8,128)(2,1)} %copy.24) | data formatting | bytes 16777216 | tf_op jit(solution)/shard_map/all_to_all | solution.py:61
  826.6 231.7 %all_to_all.37 = bf16[16,64,4096]{2,1,0:T(8,128)(2,1)} all-to-all(bf16[16,64,4096]{2,1,0:T(8,128)(2,1)} %all_to_all.31), channel_id=1, replica_groups=mesh['groups'=2,'slab'=16] {'slab'}, dimensions={0} | all-to-all | bytes 16777216 | tf_op jit(solution)/shard_map/all_to_all | solution.py:61
  1058.4 7.9 copy.27
  (3 shorter events, 0.0 us)
Async XLA Ops:
  49.2 8.2 copy-start.2
  49.2 8.7 copy-start
  49.2 305.2 %all-to-all-start = ((bf16[64,16,2,4096]{3,0,2,1:T(8,128)(2,1)}), bf16[64,16,2,4096]{3,0,2,1:T(8,128)(2,1)}, u32[]{:S(2)}, u32[]{:S(2)}) async-start(bf16[64,16,2,4096]{3,0,2,1:T(8,128)(2,1)} %copy.18), calls=%async_computation | async-start | bytes 33554432 | tf_op jit(solution)/shard_map/all_to_all | solution.py:38
  471.9 203.6 %collective-permute-start = (bf16[1024,32,128]{2,0,1:T(8,128)(2,1)}, bf16[1024,32,128]{2,0,1:T(8,128)(2,1)}, u32[]{:S(2)}, u32[]{:S(2)}) collective-permute-start(bf16[1024,32,128]{2,0,1:T(8,128)(2,1)} %fusion.21), channel_id=1, source_target_pairs={{0,2},{2,0},{1,3},{3,1},{4,6},{6,4},{5,7},{7,5},{8,10},{10,8},{9,1... | collective-permute-start | bytes 25165832 | tf_op jit(solution)/shard_map/ppermute | solution.py:16
  731.3 13.5 %collective-permute-start.1 = (bf16[1024,32,128]{2,0,1:T(8,128)(2,1)}, bf16[1024,32,128]{2,0,1:T(8,128)(2,1)}, u32[]{:S(2)}, u32[]{:S(2)}) collective-permute-start(bf16[1024,32,128]{2,0,1:T(8,128)(2,1)} %fusion.27), channel_id=1, source_target_pairs={{0,1},{1,0},{2,3},{3,2},{4,5},{5,4},{6,7},{7,6},{8,9},{9,8},{10,11... | collective-permute-start | bytes 25165832 | tf_op jit(solution)/shard_map/ppermute | solution.py:16
  778.8 8.6 copy-start.1
  778.8 8.6 copy-start.3
where the time goes:
time: 1070 us
  waiting for transfers between devices  466 us (44%)
  blocking collectives  232 us (22%)
  local copies, waits for them, and re-layouts  177 us (17%)
  matrix products  152 us (14%)
  starting transfers between devices  31.4 us (3%)
    all_to_all x1, waiting for transfers between devices, local(): lax.all_to_all(paired, 'slab', split_axis=1, concat_axis=0, tiled=True)  296 us
    all_to_all x1, blocking collectives, local(): lax.all_to_all(flattened, 'slab', split_axis=0, concat_axis=1, tiled=True)  232 us
    ppermute x2, waiting for transfers between devices, from_partner(): return lax.ppermute(block, axis, route)  171 us
    dot_general x6, matrix products, local(): jnp.einsum('rkb,kbc->rkc', crossing, weights[layer_index, 1], preferred_e...  81.4 us
    dot_general x6, matrix products, local(): jnp.einsum('rkb,kbc->rkc', current, weights[layer_index, 0], preferred_el...  70.2 us
    gather x6, local copies, waits for them, and re-layouts, local(): crossing = jnp.take(source, columns[layer_index], axis=1)  51.3 us
    another operation x2, local copies, waits for them, and re-layouts, local(): paired = jnp.stack([grouped, flipped], axis=2)  29.1 us
    ppermute x2, starting transfers between devices, from_partner(): return lax.ppermute(block, axis, route)  23.2 us
  transfers between devices with their start and end apart: 3, of which 3 were waited for; matrix products, arithmetic and copies ran while one was open for 2% of the time, Pallas kernels for 0%

commit v1 on v0

--- a/solution.py
+++ b/solution.py
@@ -35,7 +35,18 @@
     )
     flipped = flipped[:, :, ::-1].reshape(local_rows, slab_count, per_device * block_width)
     paired = jnp.stack([grouped, flipped], axis=2)
-    arrived = lax.all_to_all(paired, "slab", split_axis=1, concat_axis=0, tiled=True)
+    ways, here = (lax.axis_size("slab"), lax.axis_index("slab"))
+    width = paired.shape[1] // ways
+    shape = list(paired.shape)
+    shape[1] = width
+    height = shape[0]
+    shape[0] = height * ways
+    arrived = jnp.zeros(shape, paired.dtype)
+    for mask in range(ways):
+        part = lax.dynamic_slice_in_dim(paired, (here ^ mask) * width, width, axis=1)
+        if mask:
+            part = lax.ppermute(part, "slab", [(d, d ^ mask) for d in range(ways)])
+        arrived = lax.dynamic_update_slice_in_dim(arrived, part, (here ^ mask) * height, axis=0)
     current = arrived[:, 0, 0].reshape(-1, per_device, block_width)
     first_cross = arrived[:, 0, 1].reshape(-1, per_device, block_width)
     for layer_index in range(layer_count):

time: 1070 us -> 1260 us (1.18)
  local copies, waits for them, and re-layouts: 177 us -> 547 us
  waiting for transfers between devices: 466 us -> 319 us
  blocking collectives: 232 us -> 188 us
  starting transfers between devices: 31.4 us -> 15.3 us
  other arithmetic: 8.53 us -> 23.6 us
    dynamic_update_slice x0 -> x16, local copies, waits for them, and re-layouts: none -> 335 us  [local(): lax.dynamic_update_slice_in_dim(arrived, part, (here ^ mask) * height, ax...]
    all_to_all x1 -> x0, waiting for transfers between devices: 296 us -> none  [local(): lax.all_to_all(paired, 'slab', split_axis=1, concat_axis=0, tiled=True)]
    ppermute x0 -> x15, waiting for transfers between devices: none -> 147 us  [local(): part = lax.ppermute(part, 'slab', [(d, d ^ mask) for d in range(ways)])]
    all_to_all x1, blocking collectives: 232 us -> 188 us  [local(): lax.all_to_all(flattened, 'slab', split_axis=0, concat_axis=1, tiled=True)]
    dynamic_slice x0 -> x15, local copies, waits for them, and re-layouts: none -> 38.1 us  [local(): lax.dynamic_slice_in_dim(paired, (here ^ mask) * width, width, axis=1)]
    ppermute x0 -> x15, local copies, waits for them, and re-layouts: none -> 29.4 us  [local(): part = lax.ppermute(part, 'slab', [(d, d ^ mask) for d in range(ways)])]
    another operation x2 -> x0, local copies, waits for them, and re-layouts: 29.1 us -> none  [local(): paired = jnp.stack([grouped, flipped], axis=2)]
    ppermute x2, starting transfers between devices: 23.2 us -> 1.11 us  [from_partner(): return lax.ppermute(block, axis, route)]
  transfers between devices with their start and end apart: 3 -> 17, of which waited for: 3 -> 9; matrix products, arithmetic and copies ran while one was open for 2% -> 34% of each run, Pallas kernels for 0% -> 0%
where the time goes in v1:
time: 1260 us; the launch traced here: 1250 us
  local copies, waits for them, and re-layouts  547 us (43%)
  waiting for transfers between devices  319 us (25%)
  blocking collectives  188 us (15%)
  matrix products  152 us (12%)
  other arithmetic  23.6 us (2%)
  starting transfers between devices  15.3 us (1%)
    dynamic_update_slice x16, local copies, waits for them, and re-layouts, local(): lax.dynamic_update_slice_in_dim(arrived, part, (here ^ mask) * height, ax...  335 us
    all_to_all x1, blocking collectives, local(): lax.all_to_all(flattened, 'slab', split_axis=0, concat_axis=1, tiled=True)  188 us
    ppermute x2, waiting for transfers between devices, from_partner(): return lax.ppermute(block, axis, route)  172 us
    ppermute x15, waiting for transfers between devices, local(): part = lax.ppermute(part, 'slab', [(d, d ^ mask) for d in range(ways)])  147 us
    dot_general x6, matrix products, local(): jnp.einsum('rkb,kbc->rkc', crossing, weights[layer_index, 1], preferred_e...  79.7 us
    dot_general x6, matrix products, local(): jnp.einsum('rkb,kbc->rkc', current, weights[layer_index, 0], preferred_el...  72.4 us
    gather x6, local copies, waits for them, and re-layouts, local(): crossing = jnp.take(source, columns[layer_index], axis=1)  51.5 us
    dynamic_slice x15, local copies, waits for them, and re-layouts, local(): lax.dynamic_slice_in_dim(paired, (here ^ mask) * width, width, axis=1)  38.1 us
  transfers between devices with their start and end apart: 17, of which 9 were waited for; matrix products, arithmetic and copies ran while one was open for 34% of the time, Pallas kernels for 0%

profile of v1, /device:TPU:1, one launch (start us, length us, event | category | flops | bytes accessed | tf_op | source)
XLA Modules:
  0.0 1245.2 jit_solution(18279217723718533603)
XLA Ops:
  0.0 15.6 %copy.16 = bf16[64,65536]{0,1:T(8,128)(2,1)} copy(bf16[64,65536]{1,0:T(8,128)(2,1)} %param.6) | data formatting | bytes 16777216 | tf_op args[0]
  15.6 13.7 %rev.3 = bf16[64,1,2,8,4096]{0,4,3,2,1:T(8,128)(2,1)} reverse(bf16[64,1,2,8,4096]{0,4,3,2,1:T(8,128)(2,1)} %bitcast.114), dimensions={2} | reverse | bytes 16777216 | tf_op jit(solution)/shard_map/rev | solution.py:36
  63.7 8.8 fusion.56
  87.2 11.3 collective-permute-done.3
  102.9 45.3 %collective-permute-done.1 = bf16[64,1,2,4096]{3,0,2,1:T(8,128)(2,1)} collective-permute-done((bf16[64,1,2,4096]{3,0,2,1:T(8,128)(2,1)}, bf16[64,1,2,4096]{3,0,2,1:T(8,128)(2,1)}, u32[]{:S(2)}, u32[]{:S(2)}) %collective-permute-start.1) | collective-permute-done | bytes 1048608 | tf_op jit(solution)/shard_map/ppermute | solution.py:48
  163.7 17.9 %collective-permute-done.7 = bf16[64,1,2,4096]{3,0,2,1:T(8,128)(2,1)} collective-permute-done((bf16[64,1,2,4096]{3,0,2,1:T(8,128)(2,1)}, bf16[64,1,2,4096]{3,0,2,1:T(8,128)(2,1)}, u32[]{:S(2)}, u32[]{:S(2)}) %collective-permute-start.7) | collective-permute-done | bytes 1048608 | tf_op jit(solution)/shard_map/ppermute | solution.py:48
  182.3 23.0 %collective-permute-done.5 = bf16[64,1,2,4096]{3,0,2,1:T(8,128)(2,1)} collective-permute-done((bf16[64,1,2,4096]{3,0,2,1:T(8,128)(2,1)}, bf16[64,1,2,4096]{3,0,2,1:T(8,128)(2,1)}, u32[]{:S(2)}, u32[]{:S(2)}) %collective-permute-start.5) | collective-permute-done | bytes 1048608 | tf_op jit(solution)/shard_map/ppermute | solution.py:48
  205.8 44.3 %collective-permute-done.4 = bf16[64,1,2,4096]{3,0,2,1:T(8,128)(2,1)} collective-permute-done((bf16[64,1,2,4096]{3,0,2,1:T(8,128)(2,1)}, bf16[64,1,2,4096]{3,0,2,1:T(8,128)(2,1)}, u32[]{:S(2)}, u32[]{:S(2)}) %collective-permute-start.4) | collective-permute-done | bytes 1048608 | tf_op jit(solution)/shard_map/ppermute | solution.py:48
  258.0 22.5 %dynamic_update_slice.48 = bf16[1024,1,2,4096]{0,3,2,1:T(8,128)(2,1)} dynamic-update-slice(bf16[1024,1,2,4096]{0,3,2,1:T(8,128)(2,1)} %broadcast_in_dim.12, bf16[64,1,2,4096]{0,3,2,1:T(8,128)(2,1)S(1)} %copy-done, s32[]{:T(128)S(6)} %select_n.104, s32[]{:T(128)} %constant.3.clone.1, s32[]{:T(128)} %constant.3.clone.1, s32[]{:T(128)} %constant.3.clone.1) | dynamic-update-slice | bytes 2097156 | tf_op jit(solution)/shard_map/dynamic_update_slice | solution.py:49
  283.2 19.8 %dynamic_update_slice.49 = bf16[1024,1,2,4096]{0,3,2,1:T(8,128)(2,1)} dynamic-update-slice(bf16[1024,1,2,4096]{0,3,2,1:T(8,128)(2,1)} %dynamic_update_slice.48, bf16[64,1,2,4096]{0,3,2,1:T(8,128)(2,1)S(1)} %copy.19, s32[]{:T(128)S(6)} %select_n.106, s32[]{:T(128)} %constant.3.clone.1, s32[]{:T(128)} %constant.3.clone.1, s32[]{:T(128)} %constant.3.clone.1) | dynamic-update-slice | bytes 2097156 | tf_op jit(solution)/shard_map/dynamic_update_slice | solution.py:49
  305.0 22.5 %dynamic_update_slice.50 = bf16[1024,1,2,4096]{0,3,2,1:T(8,128)(2,1)} dynamic-update-slice(bf16[1024,1,2,4096]{0,3,2,1:T(8,128)(2,1)} %dynamic_update_slice.49, bf16[64,1,2,4096]{0,3,2,1:T(8,128)(2,1)S(1)} %copy.21, s32[]{:T(128)S(6)} %select_n.108, s32[]{:T(128)} %constant.3.clone.1, s32[]{:T(128)} %constant.3.clone.1, s32[]{:T(128)} %constant.3.clone.1) | dynamic-update-slice | bytes 2097156 | tf_op jit(solution)/shard_map/dynamic_update_slice | solution.py:49
  329.5 19.5 %dynamic_update_slice.51 = bf16[1024,1,2,4096]{0,3,2,1:T(8,128)(2,1)} dynamic-update-slice(bf16[1024,1,2,4096]{0,3,2,1:T(8,128)(2,1)} %dynamic_update_slice.50, bf16[64,1,2,4096]{0,3,2,1:T(8,128)(2,1)S(1)} %copy.23, s32[]{:T(128)S(6)} %select_n.110, s32[]{:T(128)} %constant.3.clone.1, s32[]{:T(128)} %constant.3.clone.1, s32[]{:T(128)} %constant.3.clone.1) | dynamic-update-slice | bytes 2097156 | tf_op jit(solution)/shard_map/dynamic_update_slice | solution.py:49
  351.1 22.5 %dynamic_update_slice.52 = bf16[1024,1,2,4096]{0,3,2,1:T(8,128)(2,1)} dynamic-update-slice(bf16[1024,1,2,4096]{0,3,2,1:T(8,128)(2,1)} %dynamic_update_slice.51, bf16[64,1,2,4096]{0,3,2,1:T(8,128)(2,1)S(1)} %copy.25, s32[]{:T(128)S(6)} %select_n.112, s32[]{:T(128)} %constant.3.clone.1, s32[]{:T(128)} %constant.3.clone.1, s32[]{:T(128)} %constant.3.clone.1) | dynamic-update-slice | bytes 2097156 | tf_op jit(solution)/shard_map/dynamic_update_slice | solution.py:49
  375.6 19.5 %dynamic_update_slice.53 = bf16[1024,1,2,4096]{0,3,2,1:T(8,128)(2,1)} dynamic-update-slice(bf16[1024,1,2,4096]{0,3,2,1:T(8,128)(2,1)} %dynamic_update_slice.52, bf16[64,1,2,4096]{0,3,2,1:T(8,128)(2,1)S(1)} %copy.27, s32[]{:T(128)S(6)} %select_n.114, s32[]{:T(128)} %constant.3.clone.1, s32[]{:T(128)} %constant.3.clone.1, s32[]{:T(128)} %constant.3.clone.1) | dynamic-update-slice | bytes 2097156 | tf_op jit(solution)/shard_map/dynamic_update_slice | solution.py:49
  397.2 22.5 %dynamic_update_slice.54 = bf16[1024,1,2,4096]{0,3,2,1:T(8,128)(2,1)} dynamic-update-slice(bf16[1024,1,2,4096]{0,3,2,1:T(8,128)(2,1)} %dynamic_update_slice.53, bf16[64,1,2,4096]{0,3,2,1:T(8,128)(2,1)S(1)} %copy.29, s32[]{:T(128)S(6)} %select_n.116, s32[]{:T(128)} %constant.3.clone.1, s32[]{:T(128)} %constant.3.clone.1, s32[]{:T(128)} %constant.3.clone.1) | dynamic-update-slice | bytes 2097156 | tf_op jit(solution)/shard_map/dynamic_update_slice | solution.py:49
  421.7 19.6 %dynamic_update_slice.55 = bf16[1024,1,2,4096]{0,3,2,1:T(8,128)(2,1)} dynamic-update-slice(bf16[1024,1,2,4096]{0,3,2,1:T(8,128)(2,1)} %dynamic_update_slice.54, bf16[64,1,2,4096]{0,3,2,1:T(8,128)(2,1)S(1)} %copy.31, s32[]{:T(128)S(6)} %select_n.118, s32[]{:T(128)} %constant.3.clone.1, s32[]{:T(128)} %constant.3.clone.1, s32[]{:T(128)} %constant.3.clone.1) | dynamic-update-slice | bytes 2097156 | tf_op jit(solution)/shard_map/dynamic_update_slice | solution.py:49
  443.3 22.5 %dynamic_update_slice.56 = bf16[1024,1,2,4096]{0,3,2,1:T(8,128)(2,1)} dynamic-update-slice(bf16[1024,1,2,4096]{0,3,2,1:T(8,128)(2,1)} %dynamic_update_slice.55, bf16[64,1,2,4096]{0,3,2,1:T(8,128)(2,1)S(1)} %copy.33, s32[]{:T(128)S(6)} %select_n.120, s32[]{:T(128)} %constant.3.clone.1, s32[]{:T(128)} %constant.3.clone.1, s32[]{:T(128)} %constant.3.clone.1) | dynamic-update-slice | bytes 2097156 | tf_op jit(solution)/shard_map/dynamic_update_slice | solution.py:49
  467.9 19.6 %dynamic_update_slice.57 = bf16[1024,1,2,4096]{0,3,2,1:T(8,128)(2,1)} dynamic-update-slice(bf16[1024,1,2,4096]{0,3,2,1:T(8,128)(2,1)} %dynamic_update_slice.56, bf16[64,1,2,4096]{0,3,2,1:T(8,128)(2,1)S(1)} %copy.35, s32[]{:T(128)S(6)} %select_n.122, s32[]{:T(128)} %constant.3.clone.1, s32[]{:T(128)} %constant.3.clone.1, s32[]{:T(128)} %constant.3.clone.1) | dynamic-update-slice | bytes 2097156 | tf_op jit(solution)/shard_map/dynamic_update_slice | solution.py:49
  488.5 22.6 %dynamic_update_slice.58 = bf16[1024,1,2,4096]{0,3,2,1:T(8,128)(2,1)} dynamic-update-slice(bf16[1024,1,2,4096]{0,3,2,1:T(8,128)(2,1)} %dynamic_update_slice.57, bf16[64,1,2,4096]{0,3,2,1:T(8,128)(2,1)S(1)} %copy.37, s32[]{:T(128)S(6)} %select_n.124, s32[]{:T(128)} %constant.3.clone.1, s32[]{:T(128)} %constant.3.clone.1, s32[]{:T(128)} %constant.3.clone.1) | dynamic-update-slice | bytes 2097156 | tf_op jit(solution)/shard_map/dynamic_update_slice | solution.py:49
  513.1 19.6 %dynamic_update_slice.59 = bf16[1024,1,2,4096]{0,3,2,1:T(8,128)(2,1)} dynamic-update-slice(bf16[1024,1,2,4096]{0,3,2,1:T(8,128)(2,1)} %dynamic_update_slice.58, bf16[64,1,2,4096]{0,3,2,1:T(8,128)(2,1)S(1)} %copy.39, s32[]{:T(128)S(6)} %select_n.126, s32[]{:T(128)} %constant.3.clone.1, s32[]{:T(128)} %constant.3.clone.1, s32[]{:T(128)} %constant.3.clone.1) | dynamic-update-slice | bytes 2097156 | tf_op jit(solution)/shard_map/dynamic_update_slice | solution.py:49
  534.7 22.5 %dynamic_update_slice.60 = bf16[1024,1,2,4096]{0,3,2,1:T(8,128)(2,1)} dynamic-update-slice(bf16[1024,1,2,4096]{0,3,2,1:T(8,128)(2,1)} %dynamic_update_slice.59, bf16[64,1,2,4096]{0,3,2,1:T(8,128)(2,1)S(1)} %copy.41, s32[]{:T(128)S(6)} %select_n.128, s32[]{:T(128)} %constant.3.clone.1, s32[]{:T(128)} %constant.3.clone.1, s32[]{:T(128)} %constant.3.clone.1) | dynamic-update-slice | bytes 2097156 | tf_op jit(solution)/shard_map/dynamic_update_slice | solution.py:49
  559.3 19.6 %dynamic_update_slice.61 = bf16[1024,1,2,4096]{0,3,2,1:T(8,128)(2,1)} dynamic-update-slice(bf16[1024,1,2,4096]{0,3,2,1:T(8,128)(2,1)} %dynamic_update_slice.60, bf16[64,1,2,4096]{0,3,2,1:T(8,128)(2,1)S(1)} %copy.43, s32[]{:T(128)S(6)} %select_n.130, s32[]{:T(128)} %constant.3.clone.1, s32[]{:T(128)} %constant.3.clone.1, s32[]{:T(128)} %constant.3.clone.1) | dynamic-update-slice | bytes 2097156 | tf_op jit(solution)/shard_map/dynamic_update_slice | solution.py:49
  580.9 21.7 %dynamic_update_slice.62 = bf16[1024,1,2,4096]{0,3,2,1:T(8,128)(2,1)} dynamic-update-slice(bf16[1024,1,2,4096]{0,3,2,1:T(8,128)(2,1)} %dynamic_update_slice.61, bf16[64,1,2,4096]{0,3,2,1:T(8,128)(2,1)S(1)} %copy.45, s32[]{:T(128)S(6)} %select_n.132, s32[]{:T(128)} %constant.3.clone.1, s32[]{:T(128)} %constant.3.clone.1, s32[]{:T(128)} %constant.3.clone.1) | dynamic-update-slice | bytes 2097156 | tf_op jit(solution)/shard_map/dynamic_update_slice | solution.py:49
  604.6 18.7 %dynamic_update_slice.63 = bf16[1024,1,2,4096]{0,3,2,1:T(8,128)(2,1)} dynamic-update-slice(bf16[1024,1,2,4096]{0,3,2,1:T(8,128)(2,1)} %dynamic_update_slice.62, bf16[64,1,2,4096]{0,3,2,1:T(8,128)(2,1)S(1)} %copy.47, s32[]{:T(128)S(6)} %select_n.134, s32[]{:T(128)} %constant.3.clone.1, s32[]{:T(128)} %constant.3.clone.1, s32[]{:T(128)} %constant.3.clone.1) | dynamic-update-slice | bytes 2097156 | tf_op jit(solution)/shard_map/dynamic_update_slice | solution.py:49
  623.3 11.8 fusion.92
  635.1 12.0 copy.49
  647.1 8.4 gather_fusion
  655.5 11.7 fusion.5
  667.2 14.0 %fusion.34 = bf16[1024,32,128]{2,0,1:T(8,128)(2,1)} fusion(f32[32,128]{1,0:T(8,128)S(1)} %bitcast.129, f32[32,1024,128]{2,1,0:T(8,128)} %fusion.5, bf16[1024,32,128]{0,2,1:T(8,128)(2,1)} %bitcast.123, bf16[6,2,32,128,128]{4,3,2,1,0:T(8,128)(2,1)} %param.7), kind=kOutput, calls=%fused_computation.68 | convolution fusion | flops 1090519040 | bytes 34619392 | tf_op jit(solution)/shard_map/rkb,kbc->rkc/dot_general | solution.py:63
  681.3 11.7 fusion.70
  692.9 8.6 gather_fusion.1
  701.5 13.7 %fusion.19 = bf16[1024,32,128]{2,0,1:T(8,128)(2,1)} fusion(f32[32,128]{1,0:T(8,128)S(1)} %bitcast.128, f32[32,1024,128]{2,1,0:T(8,128)} %fusion.70, bf16[32,1024,128]{2,1,0:T(8,128)(2,1)} %gather_fusion.1, pred[32]{0:T(512)(128)(4,1)S(1)} %get-tuple-element.46, bf16[6,2,32,128,128]{4,3,2,1,0:T(8,128)(2,1)} %param.7), kind=kOutput, calls=%fused_computation.63 | convolution fusion | flops 1094713344 | bytes 34619424 | tf_op jit(solution)/shard_map/rkb,kbc->rkc/dot_general | solution.py:66
  715.3 11.7 fusion.67
  726.9 170.5 %collective-permute-done.15 = bf16[1024,32,128]{2,0,1:T(8,128)(2,1)} collective-permute-done((bf16[1024,32,128]{2,0,1:T(8,128)(2,1)}, bf16[1024,32,128]{2,0,1:T(8,128)(2,1)}, u32[]{:S(2)}, u32[]{:S(2)}) %collective-permute-start.15) | collective-permute-done | bytes 8388640 | tf_op jit(solution)/shard_map/ppermute | solution.py:16
  897.4 8.6 gather_fusion.2
  906.0 13.5 %fusion.22 = bf16[1024,32,128]{2,0,1:T(8,128)(2,1)} fusion(f32[32,128]{1,0:T(8,128)S(1)} %bitcast.127, f32[32,1024,128]{2,1,0:T(8,128)} %fusion.67, bf16[32,1024,128]{2,1,0:T(8,128)(2,1)} %gather_fusion.2, pred[32]{0:T(512)(128)(4,1)S(1)} %get-tuple-element.44, bf16[6,2,32,128,128]{4,3,2,1,0:T(8,128)(2,1)} %param.7), kind=kOutput, calls=%fused_computation.64 | convolution fusion | flops 1094713344 | bytes 34619424 | tf_op jit(solution)/shard_map/rkb,kbc->rkc/dot_general | solution.py:66
  919.5 11.7 fusion.64
  931.1 8.5 gather_fusion.3
  939.7 13.5 %fusion.25 = bf16[1024,32,128]{2,0,1:T(8,128)(2,1)} fusion(f32[32,128]{1,0:T(8,128)S(1)} %bitcast.126, f32[32,1024,128]{2,1,0:T(8,128)} %fusion.64, bf16[32,1024,128]{2,1,0:T(8,128)(2,1)} %gather_fusion.3, pred[32]{0:T(512)(128)(4,1)S(1)} %get-tuple-element.42, bf16[6,2,32,128,128]{4,3,2,1,0:T(8,128)(2,1)} %param.7), kind=kOutput, calls=%fused_computation.65 | convolution fusion | flops 1094713344 | bytes 34619424 | tf_op jit(solution)/shard_map/rkb,kbc->rkc/dot_general | solution.py:66
  954.3 11.7 fusion.61
  967.4 8.8 gather_fusion.4
  976.2 13.5 %fusion.28 = bf16[1024,32,128]{2,0,1:T(8,128)(2,1)} fusion(f32[32,128]{1,0:T(8,128)S(1)} %bitcast.125, f32[32,1024,128]{2,1,0:T(8,128)} %fusion.61, bf16[32,1024,128]{2,1,0:T(8,128)(2,1)} %gather_fusion.4, pred[32]{0:T(512)(128)(4,1)S(1)} %get-tuple-element.50, bf16[6,2,32,128,128]{4,3,2,1,0:T(8,128)(2,1)} %param.7), kind=kOutput, calls=%fused_computation.66 | convolution fusion | flops 1094713344 | bytes 34619424 | tf_op jit(solution)/shard_map/rkb,kbc->rkc/dot_general | solution.py:66
  989.7 11.7 fusion.58
  1001.3 8.6 gather_fusion.5
  1009.9 13.8 %fusion.31 = bf16[1024,32,128]{2,0,1:T(8,128)(2,1)} fusion(f32[32,128]{1,0:T(8,128)S(1)} %bitcast.124, f32[32,1024,128]{2,1,0:T(8,128)} %fusion.58, bf16[32,1024,128]{2,1,0:T(8,128)(2,1)} %gather_fusion.5, pred[32]{0:T(512)(128)(4,1)S(1)} %copy-done.4, bf16[6,2,32,128,128]{4,3,2,1,0:T(8,128)(2,1)} %param.7), kind=kOutput, calls=%fused_computation.67 | convolution fusion | flops 1094713344 | bytes 34619424 | tf_op jit(solution)/shard_map/rkb,kbc->rkc/dot_general | solution.py:66
  1023.7 12.2 copy.50
  1035.9 13.3 %all_to_all.14 = bf16[16,64,4096]{2,1,0:T(8,128)(2,1)} reshape(bf16[1024,32,128]{2,1,0:T(8,128)(2,1)} %copy.50) | data formatting | bytes 16777216 | tf_op jit(solution)/shard_map/all_to_all | solution.py:72
  1049.2 187.7 %all_to_all.19 = bf16[16,64,4096]{2,1,0:T(8,128)(2,1)} all-to-all(bf16[16,64,4096]{2,1,0:T(8,128)(2,1)} %all_to_all.14), channel_id=1, replica_groups=mesh['groups'=2,'slab'=16] {'slab'}, dimensions={0} | all-to-all | bytes 16777216 | tf_op jit(solution)/shard_map/all_to_all | solution.py:72
  (77 shorter events, 118.6 us)
Async XLA Ops:
  36.9 49.6 %collective-permute-start.9 = (bf16[64,1,2,4096]{3,0,2,1:T(8,128)(2,1)}, bf16[64,1,2,4096]{3,0,2,1:T(8,128)(2,1)S(1)}, u32[]{:S(2)}, u32[]{:S(2)}) collective-permute-start(bf16[64,1,2,4096]{3,0,2,1:T(8,128)(2,1)} %copy.36), channel_id=1, source_target_pairs={{0,10},{1,11},{2,8},{3,9},{4,14},{5,15},{6,12},{7,13},{8,2},{9,3},... | collective-permute-start | bytes 3145736 | tf_op jit(solution)/shard_map/ppermute | solution.py:48
  51.8 46.6 %collective-permute-start.3 = (bf16[64,1,2,4096]{3,0,2,1:T(8,128)(2,1)}, bf16[64,1,2,4096]{3,0,2,1:T(8,128)(2,1)}, u32[]{:S(2)}, u32[]{:S(2)}) collective-permute-start(bf16[64,1,2,4096]{3,0,2,1:T(8,128)(2,1)} %copy.24), channel_id=1, source_target_pairs={{0,4},{1,5},{2,6},{3,7},{4,0},{5,1},{6,2},{7,3},{8,12},{9,13},{10,... | collective-permute-start | bytes 3145736 | tf_op jit(solution)/shard_map/ppermute | solution.py:48
  55.9 46.9 %collective-permute-start.2 = (bf16[64,1,2,4096]{3,0,2,1:T(8,128)(2,1)}, bf16[64,1,2,4096]{3,0,2,1:T(8,128)(2,1)}, u32[]{:S(2)}, u32[]{:S(2)}) collective-permute-start(bf16[64,1,2,4096]{3,0,2,1:T(8,128)(2,1)} %copy.22), channel_id=1, source_target_pairs={{0,3},{1,2},{2,1},{3,0},{4,7},{5,6},{6,5},{7,4},{8,11},{9,10},{10,... | collective-permute-start | bytes 3145736 | tf_op jit(solution)/shard_map/ppermute | solution.py:48
  60.0 88.2 %collective-permute-start.1 = (bf16[64,1,2,4096]{3,0,2,1:T(8,128)(2,1)}, bf16[64,1,2,4096]{3,0,2,1:T(8,128)(2,1)}, u32[]{:S(2)}, u32[]{:S(2)}) collective-permute-start(bf16[64,1,2,4096]{3,0,2,1:T(8,128)(2,1)} %copy.20), channel_id=1, source_target_pairs={{0,2},{1,3},{2,0},{3,1},{4,6},{5,7},{6,4},{7,5},{8,10},{9,11},{10,... | collective-permute-start | bytes 3145736 | tf_op jit(solution)/shard_map/ppermute | solution.py:48
  63.7 84.5 %collective-permute-start = (bf16[64,1,2,4096]{3,0,2,1:T(8,128)(2,1)}, bf16[64,1,2,4096]{3,0,2,1:T(8,128)(2,1)}, u32[]{:S(2)}, u32[]{:S(2)}) collective-permute-start(bf16[64,1,2,4096]{3,0,2,1:T(8,128)(2,1)} %copy.18), channel_id=1, source_target_pairs={{0,1},{1,0},{2,3},{3,2},{4,5},{5,4},{6,7},{7,6},{8,9},{9,8},{10,11... | collective-permute-start | bytes 3145736 | tf_op jit(solution)/shard_map/ppermute | solution.py:48
  86.0 165.4 %copy-start.3 = (s32[6,32]{1,0:T(8,128)S(1)}, s32[6,32]{1,0:T(8,128)}, u32[]{:S(2)}) copy-start(s32[6,32]{1,0:T(8,128)} %param.9) | copy-start | bytes 2308
  86.5 76.4 %collective-permute-start.8 = (bf16[64,1,2,4096]{3,0,2,1:T(8,128)(2,1)}, bf16[64,1,2,4096]{3,0,2,1:T(8,128)(2,1)}, u32[]{:S(2)}, u32[]{:S(2)}) collective-permute-start(bf16[64,1,2,4096]{3,0,2,1:T(8,128)(2,1)} %copy.34), channel_id=1, source_target_pairs={{0,9},{1,8},{2,11},{3,10},{4,13},{5,12},{6,15},{7,14},{8,1},{9,0},... | collective-permute-start | bytes 3145736 | tf_op jit(solution)/shard_map/ppermute | solution.py:48
  98.5 83.1 %collective-permute-start.7 = (bf16[64,1,2,4096]{3,0,2,1:T(8,128)(2,1)}, bf16[64,1,2,4096]{3,0,2,1:T(8,128)(2,1)}, u32[]{:S(2)}, u32[]{:S(2)}) collective-permute-start(bf16[64,1,2,4096]{3,0,2,1:T(8,128)(2,1)} %copy.32), channel_id=1, source_target_pairs={{0,8},{1,9},{2,10},{3,11},{4,12},{5,13},{6,14},{7,15},{8,0},{9,1},... | collective-permute-start | bytes 3145736 | tf_op jit(solution)/shard_map/ppermute | solution.py:48
  102.9 78.7 %collective-permute-start.6 = (bf16[64,1,2,4096]{3,0,2,1:T(8,128)(2,1)}, bf16[64,1,2,4096]{3,0,2,1:T(8,128)(2,1)}, u32[]{:S(2)}, u32[]{:S(2)}) collective-permute-start(bf16[64,1,2,4096]{3,0,2,1:T(8,128)(2,1)} %copy.30), channel_id=1, source_target_pairs={{0,7},{1,6},{2,5},{3,4},{4,3},{5,2},{6,1},{7,0},{8,15},{9,14},{10,... | collective-permute-start | bytes 3145736 | tf_op jit(solution)/shard_map/ppermute | solution.py:48
  148.2 57.1 %collective-permute-start.5 = (bf16[64,1,2,4096]{3,0,2,1:T(8,128)(2,1)}, bf16[64,1,2,4096]{3,0,2,1:T(8,128)(2,1)}, u32[]{:S(2)}, u32[]{:S(2)}) collective-permute-start(bf16[64,1,2,4096]{3,0,2,1:T(8,128)(2,1)} %copy.28), channel_id=1, source_target_pairs={{0,6},{1,7},{2,4},{3,5},{4,2},{5,3},{6,0},{7,1},{8,14},{9,15},{10,... | collective-permute-start | bytes 3145736 | tf_op jit(solution)/shard_map/ppermute | solution.py:48
  148.2 101.9 %collective-permute-start.4 = (bf16[64,1,2,4096]{3,0,2,1:T(8,128)(2,1)}, bf16[64,1,2,4096]{3,0,2,1:T(8,128)(2,1)}, u32[]{:S(2)}, u32[]{:S(2)}) collective-permute-start(bf16[64,1,2,4096]{3,0,2,1:T(8,128)(2,1)} %copy.26), channel_id=1, source_target_pairs={{0,5},{1,4},{2,7},{3,6},{4,1},{5,0},{6,3},{7,2},{8,13},{9,12},{10,... | collective-permute-start | bytes 3145736 | tf_op jit(solution)/shard_map/ppermute | solution.py:48
  163.0 369.8 %collective-permute-start.11 = (bf16[64,1,2,4096]{3,0,2,1:T(8,128)(2,1)}, bf16[64,1,2,4096]{3,0,2,1:T(8,128)(2,1)}, u32[]{:S(2)}, u32[]{:S(2)}) collective-permute-start(bf16[64,1,2,4096]{3,0,2,1:T(8,128)(2,1)} %copy.40), channel_id=1, source_target_pairs={{0,12},{1,13},{2,14},{3,15},{4,8},{5,9},{6,10},{7,11},{8,4},{9,5},... | collective-permute-start | bytes 3145736 | tf_op jit(solution)/shard_map/ppermute | solution.py:48
  181.6 329.4 %collective-permute-start.10 = (bf16[64,1,2,4096]{3,0,2,1:T(8,128)(2,1)}, bf16[64,1,2,4096]{3,0,2,1:T(8,128)(2,1)}, u32[]{:S(2)}, u32[]{:S(2)}) collective-permute-start(bf16[64,1,2,4096]{3,0,2,1:T(8,128)(2,1)} %copy.38), channel_id=1, source_target_pairs={{0,11},{1,10},{2,9},{3,8},{4,15},{5,14},{6,13},{7,12},{8,3},{9,2},... | collective-permute-start | bytes 3145736 | tf_op jit(solution)/shard_map/ppermute | solution.py:48
  181.6 375.7 %collective-permute-start.12 = (bf16[64,1,2,4096]{3,0,2,1:T(8,128)(2,1)}, bf16[64,1,2,4096]{3,0,2,1:T(8,128)(2,1)}, u32[]{:S(2)}, u32[]{:S(2)}) collective-permute-start(bf16[64,1,2,4096]{3,0,2,1:T(8,128)(2,1)} %copy.42), channel_id=1, source_target_pairs={{0,13},{1,12},{2,15},{3,14},{4,9},{5,8},{6,11},{7,10},{8,5},{9,4},... | collective-permute-start | bytes 3145736 | tf_op jit(solution)/shard_map/ppermute | solution.py:48
  205.3 373.6 %collective-permute-start.13 = (bf16[64,1,2,4096]{3,0,2,1:T(8,128)(2,1)}, bf16[64,1,2,4096]{3,0,2,1:T(8,128)(2,1)}, u32[]{:S(2)}, u32[]{:S(2)}) collective-permute-start(bf16[64,1,2,4096]{3,0,2,1:T(8,128)(2,1)} %copy.44), channel_id=1, source_target_pairs={{0,14},{1,15},{2,12},{3,13},{4,10},{5,11},{6,8},{7,9},{8,6},{9,7},... | collective-permute-start | bytes 3145736 | tf_op jit(solution)/shard_map/ppermute | solution.py:48
  250.1 352.4 %collective-permute-start.14 = (bf16[64,1,2,4096]{3,0,2,1:T(8,128)(2,1)}, bf16[64,1,2,4096]{3,0,2,1:T(8,128)(2,1)}, u32[]{:S(2)}, u32[]{:S(2)}) collective-permute-start(bf16[64,1,2,4096]{3,0,2,1:T(8,128)(2,1)} %copy.46), channel_id=1, source_target_pairs={{0,15},{1,14},{2,13},{3,12},{4,11},{5,10},{6,9},{7,8},{8,7},{9,6},... | collective-permute-start | bytes 3145736 | tf_op jit(solution)/shard_map/ppermute | solution.py:48
  252.0 6.0 copy-start
  252.0 28.5 %copy-start.1 = (f32[6,4096]{1,0:T(8,128)S(1)}, f32[6,4096]{1,0:T(8,128)}, u32[]{:S(2)}) copy-start(f32[6,4096]{1,0:T(8,128)} %param.8) | copy-start | bytes 294916
  715.2 182.2 %collective-permute-start.15 = (bf16[1024,32,128]{2,0,1:T(8,128)(2,1)}, bf16[1024,32,128]{2,0,1:T(8,128)(2,1)}, u32[]{:S(2)}, u32[]{:S(2)}) collective-permute-start(bf16[1024,32,128]{2,0,1:T(8,128)(2,1)} %fusion.19), channel_id=1, source_target_pairs={{0,2},{2,0},{1,3},{3,1},{4,6},{6,4},{5,7},{7,5},{8,10},{10,8},{9,1... | collective-permute-start | bytes 25165832 | tf_op jit(solution)/shard_map/ppermute | solution.py:16
  953.2 14.2 %collective-permute-start.16 = (bf16[1024,32,128]{2,0,1:T(8,128)(2,1)}, bf16[1024,32,128]{2,0,1:T(8,128)(2,1)}, u32[]{:S(2)}, u32[]{:S(2)}) collective-permute-start(bf16[1024,32,128]{2,0,1:T(8,128)(2,1)} %fusion.25), channel_id=1, source_target_pairs={{0,1},{1,0},{2,3},{3,2},{4,5},{5,4},{6,7},{7,6},{8,9},{9,8},{10,11... | collective-permute-start | bytes 25165832 | tf_op jit(solution)/shard_map/ppermute | solution.py:16
  1001.3 8.6 copy-start.2
  1001.3 8.6 copy-start.4
